TPU v7x, 512 devices: a whole 4x8x8 slice. The times are simulated.
512 devices in a mesh: req: 32 (over z, x), head: 16 (over y, core).
Axes of the slice: x: 4, y: 8, z: 8, core: 2. Of those that a mesh axis runs over, the one named last changes fastest.
Arguments:
- suffix_embeddings: bfloat16 [1024, 16, 4096], P('req', None, 'head'), may hold values from -6 to 6
- suffix_extents: int32 [1024], replicated, may hold values from 4 to 16, as said below
- memory_line_pointer: int32 [1024], replicated, may hold values from 0 to 1023, as said below
- previous_token_store: bfloat16 [1024, 4096], P('req', 'head'), may hold values from -6 to 6
- stored_memories: bfloat16 [1024, 64, 4096], P('req', 'head'), may hold values from -4 to 4
- blend_fractions: float32 [4, 4096], replicated, may hold values from 0 to 1
- acceptor_linear: bfloat16 [4096, 4096], P('req', 'head'), may hold values from -0.09375 to 0.09375
- address_linear: bfloat16 [4096, 4096], P('req', 'head'), may hold values from -0.09375 to 0.09375
- payload_linear: bfloat16 [4096, 4096], P('req', 'head'), may hold values from -0.09375 to 0.09375
- fading_baseline: float32 [4096], P('head'), may hold values from -5 to 0
- fading_bottleneck_down: bfloat16 [4096, 128], replicated, may hold values from -0.09375 to 0.09375
- fading_bottleneck_up: bfloat16 [128, 4096], P(None, 'head'), may hold values from -0.5 to 0.5
- self_reward: float32 [4096], P('head'), may hold values from -3 to 3
- team_normalizer_gain: float32 [4096], P('head'), may hold values from 0.5 to 1.5
Outputs:
- mixed_out: bfloat16 [1024, 16, 4096], P('req', None, 'head')
- new_state: bfloat16 [1024, 64, 4096], P('req', 'head')
- new_shift: bfloat16 [1024, 4096], P('req', 'head')
Inputs may be any that keep to these rules, and one draw needn't show every extreme that they name: `suffix_extents`: some request has exactly 16 live tokens and some has 4. `memory_line_pointer`: A permutation of the cache rows; rows r with equal r // 32 form one owner. For each serving group (the 32 requests s with equal s // 32) and each owner, either exactly 2 or none of the group's requests have their row at that owner.
All inputs are finite; a program needn't handle non-finite values.
Results may differ from a plain program's by a relative error of at most 0.0083.
Values may be sent and summed in bfloat16 or wider, within the bound.
A program may use at most 128 MiB of HBM per device.

v0:
```python
import math

import jax
import jax.numpy as jnp
from jax import lax
from jax.sharding import PartitionSpec as P

BL = 8
TEAM_BREADTH = 64


EPS = 0.00064


def in_one_piece(arrays, axis, dim, along):
    ends, at = ([], 0)
    for a in arrays[:-1]:
        at += a.shape[along]
        ends.append(at)
    both = jnp.concatenate(arrays, axis=along)
    return tuple(jnp.split(lax.all_gather(both, axis, axis=dim, tiled=True), ends, axis=along))


def side_by_side(arrays, axis, split_dim, concat_dim, along):
    widths = [math.prod(a.shape[along:]) for a in arrays]
    both = jnp.concatenate(
        [a.reshape(*a.shape[:along], w) for a, w in zip(arrays, widths)], axis=along
    )
    filled = lax.all_to_all(both, axis, split_axis=split_dim, concat_axis=concat_dim, tiled=True)
    blocks = jnp.split(filled, [sum(widths[:k]) for k in range(1, len(widths))], axis=along)
    return tuple(
        (b.reshape(*filled.shape[:along], *a.shape[along:]) for a, b in zip(arrays, blocks))
    )


def place_rows(source, position, total):
    blank = jnp.zeros((total,) + source.shape[1:], source.dtype)
    return blank.at[position].set(source)


def add_rows(source, weight_piece):
    return jnp.dot(source, weight_piece, preferred_element_type=jnp.float32)


def blockwise_update(
    acceptor_entries,
    address_entries,
    payload_array,
    fading_exponent,
    reward_by_team,
    starting_memory,
):
    items_count, length, device_teams, head_width = acceptor_entries.shape
    blocks = length // BL
    strict = jnp.arange(BL)[:, None] > jnp.arange(BL)[None, :]
    highest = lax.Precision.HIGHEST

    def by_blocks(array_in):
        return jnp.moveaxis(
            array_in.reshape(items_count, blocks, BL, device_teams, head_width), 1, 0
        )

    def advance(evolving_memory, inputs):
        acceptor_piece = inputs[0].astype(jnp.float32)
        address_piece = inputs[1].astype(jnp.float32)
        value_portion = inputs[2].astype(jnp.float32)
        decay_part = inputs[3]
        summed = jnp.cumsum(decay_part, axis=1)
        before = summed - decay_part
        forwarded_outer = jnp.einsum(
            "nthi,nhij->nthj", acceptor_piece * jnp.exp(before), evolving_memory, precision=highest
        )
        exponent = jnp.where(
            strict[None, :, :, None, None], before[:, :, None] - summed[:, None, :], -jnp.inf
        )
        scores = jnp.einsum(
            "nthi,nshi,ntshi->ntsh",
            acceptor_piece,
            address_piece,
            jnp.exp(exponent),
            precision=highest,
        )
        within_outer = jnp.einsum("ntsh,nshj->nthj", scores, value_portion, precision=highest)
        reward_outer = (
            jnp.sum(acceptor_piece * reward_by_team * address_piece, axis=-1, keepdims=True)
            * value_portion
        )
        closing_sum = summed[:, -1]
        carried = address_piece * jnp.exp(closing_sum[:, None] - summed)
        evolving_memory = jnp.exp(closing_sum)[..., None] * evolving_memory + jnp.einsum(
            "nshi,nshj->nhij", carried, value_portion, precision=highest
        )
        return (evolving_memory, forwarded_outer + within_outer + reward_outer)

    final_memory, produced_outputs = lax.scan(
        advance,
        starting_memory,
        (
            by_blocks(acceptor_entries),
            by_blocks(address_entries),
            by_blocks(payload_array),
            by_blocks(fading_exponent),
        ),
    )
    produced_outputs = jnp.moveaxis(produced_outputs, 0, 1).reshape(
        items_count, length, device_teams, head_width
    )
    return (produced_outputs, final_memory)


def decay_recurrence(
    acceptor_entries,
    address_entries,
    payload_array,
    low_rank_delta,
    request_lengths,
    starting_memory,
    fading_baseline,
    fading_bottleneck_up,
    self_reward,
):
    items_count, length, local_width = acceptor_entries.shape
    device_teams = local_width // TEAM_BREADTH
    alive_mask = (jnp.arange(length, dtype=jnp.int32)[None, :] < request_lengths[:, None])[
        ..., None
    ]
    fading_exponent = fading_baseline + jnp.dot(
        low_rank_delta.reshape(items_count * length, -1),
        fading_bottleneck_up,
        preferred_element_type=jnp.float32,
    ).reshape(items_count, length, local_width)
    fading_exponent = jnp.where(alive_mask, -jnp.exp(fading_exponent), jnp.zeros((), jnp.float32))
    address_entries = jnp.where(alive_mask, address_entries, jnp.zeros((), jnp.bfloat16))
    shaped = (items_count, length, device_teams, TEAM_BREADTH)
    start_state = starting_memory.astype(jnp.float32).reshape(
        items_count, device_teams, TEAM_BREADTH, TEAM_BREADTH
    )
    return blockwise_update(
        acceptor_entries.reshape(shaped),
        address_entries.reshape(shaped),
        payload_array.reshape(shaped),
        fading_exponent.reshape(shaped),
        self_reward.reshape(device_teams, TEAM_BREADTH),
        start_state,
    )


def group_norm(outputs, gain_heads, alive_mask):
    center = outputs - jnp.mean(outputs, axis=-1, keepdims=True)
    spread = jnp.mean(center * center, axis=-1, keepdims=True)
    normed = center * lax.rsqrt(spread + EPS) * gain_heads
    return jnp.where(alive_mask[..., None, None], normed, jnp.zeros((), jnp.float32))


def on_device(
    suffix_embeddings,
    suffix_extents,
    memory_line_pointer,
    previous_token_store,
    stored_memories,
    blend_fractions,
    acceptor_linear,
    address_linear,
    payload_linear,
    fading_baseline,
    fading_bottleneck_down,
    fading_bottleneck_up,
    self_reward,
    team_normalizer_gain,
):
    rows_here, length, local_width = suffix_embeddings.shape
    groups = lax.axis_size("req")
    group_index = lax.axis_index("req")
    device_teams = local_width // TEAM_BREADTH
    slot_count = 2 * rows_here // groups
    buffer_rows = groups * slot_count
    owners = (memory_line_pointer // rows_here).reshape(groups, rows_here)
    earlier = (
        jnp.arange(rows_here, dtype=jnp.int32)[:, None]
        > jnp.arange(rows_here, dtype=jnp.int32)[None, :]
    )
    matches = (owners[:, :, None] == owners[:, None, :]) & earlier[None]
    slot_rank = jnp.sum(matches.astype(jnp.int32), axis=2)
    send_all = owners * slot_count + slot_rank
    receive_all = (jnp.arange(groups, dtype=jnp.int32)[:, None] * slot_count + slot_rank).reshape(
        -1
    )
    send_slot = lax.dynamic_index_in_dim(send_all, group_index, 0, keepdims=False)
    group_length_list = lax.dynamic_index_in_dim(
        suffix_extents.reshape(groups, rows_here), group_index, 0, keepdims=False
    )
    local_rows = group_index * rows_here + jnp.arange(rows_here, dtype=jnp.int32)
    owned_by = memory_line_pointer[None, :] == local_rows[:, None]
    row_slot = jnp.sum(jnp.where(owned_by, receive_all[None, :], 0), axis=1)
    alive_mask = jnp.arange(length, dtype=jnp.int32)[None, :] < group_length_list[:, None]
    gain_heads = team_normalizer_gain.reshape(device_teams, TEAM_BREADTH)
    got_state, got_shift = (
        lax.all_to_all(
            place_rows(stored_memories, row_slot, buffer_rows),
            "req",
            split_axis=0,
            concat_axis=0,
            tiled=True,
        ),
        lax.all_to_all(
            place_rows(previous_token_store, row_slot, buffer_rows),
            "req",
            split_axis=0,
            concat_axis=0,
            tiled=True,
        ),
    )
    earlier_state = got_state[send_slot]
    prior_shift = got_shift[send_slot]
    extended = jnp.concatenate([prior_shift[:, None, :], suffix_embeddings], axis=1)
    gathered = lax.all_gather(extended, "head", axis=2, tiled=True)
    current = gathered[:, 1:].astype(jnp.float32)
    previous = gathered[:, :-1].astype(jnp.float32)

    def mixed_input(branch):
        return (
            (current + (previous - current) * blend_fractions[branch])
            .astype(jnp.bfloat16)
            .reshape(rows_here * length, -1)
        )

    recept_in = mixed_input(0)
    key_in = mixed_input(1)
    value_in = mixed_input(2)
    pieces = in_one_piece((acceptor_linear, address_linear, payload_linear), "req", 0, 1)
    acceptor_entries = add_rows(recept_in, pieces[0])
    address_entries = add_rows(key_in, pieces[1])
    payload_array = add_rows(value_in, pieces[2])
    shaped = (rows_here, length, local_width)
    acceptor_entries = acceptor_entries.astype(jnp.bfloat16).reshape(shaped)
    address_entries = address_entries.astype(jnp.bfloat16).reshape(shaped)
    payload_array = payload_array.astype(jnp.bfloat16).reshape(shaped)
    low_rank_delta = (
        jnp.tanh(
            jnp.dot(mixed_input(3), fading_bottleneck_down, preferred_element_type=jnp.float32)
        )
        .astype(jnp.bfloat16)
        .reshape(rows_here, length, -1)
    )
    last_token = suffix_embeddings[jnp.arange(rows_here, dtype=jnp.int32), group_length_list - 1]
    outputs, final_memory = decay_recurrence(
        acceptor_entries,
        address_entries,
        payload_array,
        low_rank_delta,
        group_length_list,
        earlier_state,
        fading_baseline,
        fading_bottleneck_up,
        self_reward,
    )
    state_rows = final_memory.reshape(rows_here, device_teams, TEAM_BREADTH * TEAM_BREADTH).astype(
        jnp.bfloat16
    )
    back_state, back_shift = side_by_side(
        (
            place_rows(state_rows, send_slot, buffer_rows),
            place_rows(last_token, send_slot, buffer_rows),
        ),
        "req",
        0,
        0,
        1,
    )
    new_state = back_state[row_slot]
    new_shift = back_shift[row_slot]
    mixed_out = group_norm(outputs, gain_heads, alive_mask).astype(jnp.bfloat16).reshape(shaped)
    return (mixed_out, new_state, new_shift)


def solution(mesh):
    placed = (
        P("req", None, "head"),
        P(),
        P(),
        P("req", "head"),
        P("req", "head", None),
        P(),
        P("req", "head"),
        P("req", "head"),
        P("req", "head"),
        P("head"),
        P(),
        P(None, "head"),
        P("head"),
        P("head"),
    )
    return jax.shard_map(
        on_device,
        mesh=mesh,
        in_specs=placed,
        out_specs=(P("req", None, "head"), P("req", "head", None), P("req", "head")),
        check_vma=False,
    )
```

profile of v0, /device:TPU:4, one launch (start us, length us, event | category | flops | bytes accessed | tf_op | source)
XLA Modules:
  0.0 333.5 jit_solution(13841216292693385504)
XLA Ops:
  12.3 13.4 %all-to-all-start.1 = ((bf16[32,2,256]{2,1,0:T(2,128)(2,1)}), bf16[32,2,256]{2,1,0:T(2,128)(2,1)S(1)}, u32[]{:S(2)}, u32[]{:S(2)}) async-start(bf16[32,2,256]{2,1,0:T(2,128)(2,1)} %all_to_all.18), calls=%async_computation.1 | async-start | bytes 65536 | tf_op jit(solution)/shard_map/all_to_all | solution.py:205
  25.8 7.8 %all-to-all-done.1 = bf16[32,2,256]{2,1,0:T(2,128)(2,1)S(1)} async-done(((bf16[32,2,256]{2,1,0:T(2,128)(2,1)}), bf16[32,2,256]{2,1,0:T(2,128)(2,1)S(1)}, u32[]{:S(2)}, u32[]{:S(2)}) %all-to-all-start.1) | async-done | bytes 32800 | tf_op jit(solution)/shard_map/all_to_all | solution.py:205
  37.8 2.3 broadcast.170.clone
  40.2 4.7 %scatter_fusion = bf16[64,4,4096]{2,1,0:T(4,128)(2,1)} fusion(bf16[64,4,4096]{2,1,0:T(4,128)(2,1)} %broadcast.170.clone, s32[32]{0:T(128)S(1)} %get-tuple-element.97, bf16[32,4,4096]{2,1,0:T(4,128)(2,1)S(1)} %copy-done.4), kind=kCustom, calls=%fused_computation.5 | custom fusion | bytes 3145856 | tf_op jit(solution)/shard_map/scatter | solution.py:38
  44.9 5.9 %all-to-all-start = ((bf16[64,4,4096]{2,1,0:T(4,128)(2,1)}), bf16[64,4,4096]{2,1,0:T(4,128)(2,1)S(1)}, u32[]{:S(2)}, u32[]{:S(2)}) async-start(bf16[64,4,4096]{2,1,0:T(4,128)(2,1)} %scatter_fusion), calls=%async_computation | async-start | bytes 4194304 | tf_op jit(solution)/shard_map/all_to_all | solution.py:198
  53.0 46.6 %all-to-all-done = bf16[64,4,4096]{2,1,0:T(4,128)(2,1)S(1)} async-done(((bf16[64,4,4096]{2,1,0:T(4,128)(2,1)}), bf16[64,4,4096]{2,1,0:T(4,128)(2,1)S(1)}, u32[]{:S(2)}, u32[]{:S(2)}) %all-to-all-start) | async-done | bytes 2097184 | tf_op jit(solution)/shard_map/all_to_all | solution.py:198
  99.6 2.4 gather_fusion
  101.9 4.5 %reshape.284 = f32[32,4,64,64]{3,2,1,0:T(8,128)} reshape(bf16[32,4,4096]{2,1,0:T(4,128)(2,1)} %gather_fusion) | data formatting | bytes 3145728 | tf_op jit(solution)/shard_map/convert_element_type | solution.py:135
  106.4 11.7 %fusion.33 = (bf16[32,16,4096]{2,1,0:T(8,128)(2,1)}, bf16[32,16,4096]{2,1,0:T(8,128)(2,1)}, bf16[32,16,4096]{2,1,0:T(8,128)(2,1)}, bf16[32,16,4096]{2,1,0:T(8,128)(2,1)}) fusion(f32[4096]{0:T(1024)S(1)} %bitcast.154, bf16[32,17,4096]{2,1,0:T(8,128)(2,1)} %all-gather.3.cloned.1.call-done, f32[4096]{0:T(1024)S(1)} %bitcast.157, f32[4096]{0:T(1024)S(1)} %bitcast.155, ...), kind=kLoop, calls=%fused_computation.60 | loop fusion | flops 31457280 | bytes 25231360 | tf_op jit(solution)/shard_map/convert_element_type | solution.py:223
  118.1 3.6 %fusion.50 = f32[512,256]{1,0:T(8,128)S(1)} fusion(bf16[128,256]{1,0:T(8,128)(2,1)S(1)} %copy-done.5, bf16[512,4096]{1,0:T(8,128)(2,1)} %bitcast.147, bf16[4096,128]{1,0:T(8,128)(2,1)S(1)} %copy-done), kind=kOutput, calls=%fused_computation.73 | convolution fusion | flops 570490880 | bytes 5832704 | tf_op jit(solution)/shard_map/dot_general | solution.py:127
  123.4 63.8 %all-gather.5.cloned.1.call-done = bf16[4096,768]{1,0:T(8,128)(2,1)} async-done(((bf16[128,768]{1,0:T(8,128)(2,1)}), bf16[4096,768]{1,0:T(8,128)(2,1)}) %all-gather.5.cloned.1.call-update) | async-done | bytes 6291472 | tf_op jit(solution)/shard_map/all_gather | solution.py:21
  187.2 4.1 %fusion.40 = bf16[512,256]{1,0:T(8,128)(2,1)S(1)} fusion(bf16[512,4096]{1,0:T(8,128)(2,1)} %bitcast.153, bf16[4096,768]{1,0:T(8,128)(2,1)} %all-gather.5.cloned.1.call-done), kind=kOutput, calls=%fused_computation.68 | convolution fusion | flops 1073872896 | bytes 6553600 | tf_op jit(solution)/shard_map/dot_general | solution.py:42
  191.7 4.1 %fusion.46 = bf16[512,256]{1,0:T(8,128)(2,1)S(1)} fusion(bf16[512,4096]{1,0:T(8,128)(2,1)} %bitcast.152, bf16[4096,768]{1,0:T(8,128)(2,1)} %all-gather.5.cloned.1.call-done), kind=kOutput, calls=%fused_computation.70 | convolution fusion | flops 1073872896 | bytes 6553600 | tf_op jit(solution)/shard_map/dot_general | solution.py:42
  196.2 4.1 %fusion.43 = bf16[512,256]{1,0:T(8,128)(2,1)S(1)} fusion(bf16[512,4096]{1,0:T(8,128)(2,1)} %bitcast.151, bf16[4096,768]{1,0:T(8,128)(2,1)} %all-gather.5.cloned.1.call-done), kind=kOutput, calls=%fused_computation.69 | convolution fusion | flops 1073872896 | bytes 6553600 | tf_op jit(solution)/shard_map/dot_general | solution.py:42
  200.6 41.5 %while.13 = (s32[]{:T(128)}, f32[32,4,64,64]{3,2,1,0:T(8,128)}, f32[2,32,8,4,64]{4,2,3,1,0:T(8,128)}, f32[2,32,8,4,64]{4,2,3,1,0:T(8,128)}, bf16[2,32,8,4,64]{4,...) while((s32[]{:T(128)}, f32[32,4,64,64]{3,2,1,0:T(8,128)}, ...), condition=%wide.region_7.8_spmd.clone, body=%wide.region_4.7_spmd.clone.sunk | while | flops 112125056 | bytes 33593624 | solution.py:95
  205.5 2.8 fusion.91
  209.0 3.6 %fusion.92 = f32[32,8,4,64]{3,1,2,0:T(8,128)S(1)} fusion(f32[32,8,4,64]{3,1,2,0:T(8,128)S(1)} %convolution_bitcast_fusion.3, f32[32,4,64,64]{3,2,1,0:T(8,128)S(1)} %copy-done.2, f32[32,8,4,64]{3,1,2,0:T(8,128)S(1)} %fusion.90, bf16[2,32,8,4,64]{4,2,3,1,0:T(8,128)(2,1)S(1)} %get-tuple-element.178, s32[]{:T(128)} %get-tuple-element.162), kind=kOutput, calls=%fused_computation.20.clone.1 | convolution fusion | flops 50528256 | bytes 5767172 | tf_op jit(solution)/shard_map/while/body/eval_jaxpr/nthi,nhij->nthj/dot_general | solution.py:70
  213.8 7.5 %multiply_add_fusion.3 = f32[32,4,64,64]{3,2,1,0:T(8,128)} fusion(f32[32,4,64,64]{3,2,1,0:T(8,128)} %get-tuple-element.163, f32[32,4,64]{2,1,0:T(4,128)S(1)} %exp.48, f32[32,8,4,64]{3,1,2,0:T(8,128)S(1)} %reduce_window_sum.13, f32[32,4,64]{2,1,0:T(4,128)S(1)} %bitcast.149, bf16[2,32,8,4,64]{4,2,3,1,0:T(8,128)(2,1)S(1)} %get-tuple-element.177, ...), kind=kOutput, calls=%fused_computation.14.clone.1 | convolution fusion | flops 51576832 | bytes 7472128 | tf_op jit(solution)/shard_map/while/body/eval_jaxpr/nshi,nshj->nhij/dot_general | solution.py:90
  226.0 2.8 fusion.91
  229.5 3.6 %fusion.92 = f32[32,8,4,64]{3,1,2,0:T(8,128)S(1)} fusion(f32[32,8,4,64]{3,1,2,0:T(8,128)S(1)} %convolution_bitcast_fusion.3, f32[32,4,64,64]{3,2,1,0:T(8,128)S(1)} %copy-done.2, f32[32,8,4,64]{3,1,2,0:T(8,128)S(1)} %fusion.90, bf16[2,32,8,4,64]{4,2,3,1,0:T(8,128)(2,1)S(1)} %get-tuple-element.178, s32[]{:T(128)} %get-tuple-element.162), kind=kOutput, calls=%fused_computation.20.clone.1 | convolution fusion | flops 50528256 | bytes 5767172 | tf_op jit(solution)/shard_map/while/body/eval_jaxpr/nthi,nhij->nthj/dot_general | solution.py:70
  234.4 7.5 %multiply_add_fusion.3 = f32[32,4,64,64]{3,2,1,0:T(8,128)} fusion(f32[32,4,64,64]{3,2,1,0:T(8,128)} %get-tuple-element.163, f32[32,4,64]{2,1,0:T(4,128)S(1)} %exp.48, f32[32,8,4,64]{3,1,2,0:T(8,128)S(1)} %reduce_window_sum.13, f32[32,4,64]{2,1,0:T(4,128)S(1)} %bitcast.149, bf16[2,32,8,4,64]{4,2,3,1,0:T(8,128)(2,1)S(1)} %get-tuple-element.177, ...), kind=kOutput, calls=%fused_computation.14.clone.1 | convolution fusion | flops 51576832 | bytes 7472128 | tf_op jit(solution)/shard_map/while/body/eval_jaxpr/nshi,nshj->nhij/dot_general | solution.py:90
  242.1 2.7 convert_element_type.79
  248.9 3.2 concatenate.19
  252.1 5.0 %pad_maximum_fusion = bf16[32,2,16640]{2,1,0:T(2,128)(2,1)} fusion(bf16[32,2,256]{2,1,0:T(2,128)(2,1)S(1)} %concatenate.21, bf16[32,2,16384]{2,1,0:T(2,128)(2,1)} %concatenate.19), kind=kLoop, calls=%fused_computation.61 | loop fusion | flops 4259840 | bytes 4259840 | tf_op jit(solution)/shard_map/concatenate | solution.py:26
  257.1 7.3 %all-to-all-start.2 = ((bf16[32,2,16640]{2,1,0:T(2,128)(2,1)}), bf16[32,2,16640]{2,1,0:T(2,128)(2,1)S(1)}, u32[]{:S(2)}, u32[]{:S(2)}) async-start(bf16[32,2,16640]{2,1,0:T(2,128)(2,1)} %pad_maximum_fusion), calls=%async_computation.2 | async-start | bytes 4259840 | tf_op jit(solution)/shard_map/all_to_all | solution.py:29
  267.8 2.6 mul.138
  272.3 2.6 sub.65
  278.1 2.0 select_convert_fusion
  280.1 34.4 %all-to-all-done.2 = bf16[32,2,16640]{2,1,0:T(2,128)(2,1)S(1)} async-done(((bf16[32,2,16640]{2,1,0:T(2,128)(2,1)}), bf16[32,2,16640]{2,1,0:T(2,128)(2,1)S(1)}, u32[]{:S(2)}, u32[]{:S(2)}) %all-to-all-start.2) | async-done | bytes 2129952 | tf_op jit(solution)/shard_map/all_to_all | solution.py:29
  314.5 2.2 all_to_all.22
  318.3 2.8 reshape.283
  321.1 3.9 %gather_fusion.2 = bf16[32,4,4096]{2,1,0:T(4,128)(2,1)} fusion(bf16[64,4,4096]{2,1,0:T(4,128)(2,1)} %reshape.283, s32[1024]{0:T(1024)S(1)} %pad_clamp_fusion), kind=kCustom, calls=%fused_computation.3 | custom fusion | bytes 2097280 | tf_op jit(solution)/shard_map/gather | solution.py:270
  (113 shorter events, 42.4 us)
Async XLA Ops:
  7.2 111.0 %copy-start = (bf16[4096,128]{1,0:T(8,128)(2,1)S(1)}, bf16[4096,128]{1,0:T(8,128)(2,1)}, u32[]{:S(2)}) copy-start(bf16[4096,128]{1,0:T(8,128)(2,1)} %param.26) | copy-start | bytes 3145732
  7.2 33.0 %copy-start.4 = (bf16[32,4,4096]{2,1,0:T(4,128)(2,1)S(1)}, bf16[32,4,4096]{2,1,0:T(4,128)(2,1)}, u32[]{:S(2)}) copy-start(bf16[32,4,4096]{2,1,0:T(4,128)(2,1)} %param.20) | copy-start | bytes 3145732
  12.3 21.3 %all-to-all-start.1 = ((bf16[32,2,256]{2,1,0:T(2,128)(2,1)}), bf16[32,2,256]{2,1,0:T(2,128)(2,1)S(1)}, u32[]{:S(2)}, u32[]{:S(2)}) async-start(bf16[32,2,256]{2,1,0:T(2,128)(2,1)} %all_to_all.18), calls=%async_computation.1 | async-start | bytes 65536 | tf_op jit(solution)/shard_map/all_to_all | solution.py:205
  25.7 80.7 %all-gather.3.cloned.1.call-start = ((), (), s32[]{:S(2)}) async-start(), calls=%async_computation.3 | async-start | bytes 6684672 | tf_op jit(solution)/shard_map/all_gather | solution.py:216
  36.2 151.0 %all-gather.5.cloned.1.call-start = ((), (), s32[]{:S(2)}) async-start(), calls=%async_computation.4 | async-start | bytes 6488064 | tf_op jit(solution)/shard_map/all_gather | solution.py:21
  40.2 10.6 %copy-start.9 = (f32[256]{0:T(256)S(1)}, f32[256]{0:T(256)}, u32[]{:S(2)}) copy-start(f32[256]{0:T(256)} %param.25) | copy-start | bytes 3076
  40.2 12.7 %copy-start.6 = (f32[4,4096]{1,0:T(4,128)S(1)}, f32[4,4096]{1,0:T(4,128)}, u32[]{:S(2)}) copy-start(f32[4,4096]{1,0:T(4,128)} %param.21) | copy-start | bytes 196612
  44.9 54.7 %all-to-all-start = ((bf16[64,4,4096]{2,1,0:T(4,128)(2,1)}), bf16[64,4,4096]{2,1,0:T(4,128)(2,1)S(1)}, u32[]{:S(2)}, u32[]{:S(2)}) async-start(bf16[64,4,4096]{2,1,0:T(4,128)(2,1)} %scatter_fusion), calls=%async_computation | async-start | bytes 4194304 | tf_op jit(solution)/shard_map/all_to_all | solution.py:198
  106.4 11.7 %copy-start.5 = (bf16[128,256]{1,0:T(8,128)(2,1)S(1)}, bf16[128,256]{1,0:T(8,128)(2,1)}, u32[]{:S(2)}) copy-start(bf16[128,256]{1,0:T(8,128)(2,1)} %param.27) | copy-start | bytes 196612
  196.1 4.5 %copy-start.7 = (f32[256]{0:T(256)S(1)}, f32[256]{0:T(256)}, u32[]{:S(2)}) copy-start(f32[256]{0:T(256)} %param.28) | copy-start | bytes 3076
  205.4 3.6 %copy-start.2 = (f32[32,4,64,64]{3,2,1,0:T(8,128)S(1)}, f32[32,4,64,64]{3,2,1,0:T(8,128)}, u32[]{:S(2)}) copy-start(f32[32,4,64,64]{3,2,1,0:T(8,128)} %get-tuple-element.163) | copy-start | bytes 6291460 | tf_op jit(solution)/shard_map/while
  225.9 3.6 %copy-start.2 = (f32[32,4,64,64]{3,2,1,0:T(8,128)S(1)}, f32[32,4,64,64]{3,2,1,0:T(8,128)}, u32[]{:S(2)}) copy-start(f32[32,4,64,64]{3,2,1,0:T(8,128)} %get-tuple-element.163) | copy-start | bytes 6291460 | tf_op jit(solution)/shard_map/while
  252.1 12.4 %copy-start.3 = (f32[2,32,8,4,64]{4,2,3,1,0:T(8,128)S(1)}, f32[2,32,8,4,64]{4,2,3,1,0:T(8,128)}, u32[]{:S(2)}) copy-start(f32[2,32,8,4,64]{4,2,3,1,0:T(8,128)} %get-tuple-element.51) | copy-start | bytes 1572868
  257.1 57.4 %all-to-all-start.2 = ((bf16[32,2,16640]{2,1,0:T(2,128)(2,1)}), bf16[32,2,16640]{2,1,0:T(2,128)(2,1)S(1)}, u32[]{:S(2)}, u32[]{:S(2)}) async-start(bf16[32,2,16640]{2,1,0:T(2,128)(2,1)} %pad_maximum_fusion), calls=%async_computation.2 | async-start | bytes 4259840 | tf_op jit(solution)/shard_map/all_to_all | solution.py:29
  267.8 10.2 %copy-start.8 = (f32[256]{0:T(256)S(1)}, f32[256]{0:T(256)}, u32[]{:S(2)}) copy-start(f32[256]{0:T(256)} %param.29) | copy-start | bytes 3076
  316.7 1.6 slice-start
  316.7 9.5 %copy-start.1 = (bf16[4096,128]{1,0:T(8,128)(2,1)S(1)}, bf16[4096,128]{1,0:T(8,128)(2,1)}, u32[]{:S(2)}) copy-start(bf16[4096,128]{1,0:T(8,128)(2,1)} %param.26) | copy-start | bytes 3145732
  316.7 8.3 %slice-start.1 = ((bf16[64,16640]{1,0:T(8,128)(2,1)}), bf16[64,256]{1,0:T(8,128)(2,1)S(1)}, s32[]{:S(2)}) async-start(bf16[64,16640]{1,0:T(8,128)(2,1)} %all_to_all.22), calls=%async_computation.6 | async-start | bytes 65536 | tf_op jit(solution)/shard_map/split | solution.py:30
Sparse Core Ops, SparseCore 0:
  36.3 55.3 all-gather.2
  95.5 91.6 all-gather.4
where the time goes:
time: 338 us; the launch traced here: 334 us
  waiting for transfers between devices  153 us (45%)
  local copies, waits for them, and re-layouts  54.7 us (16%)
  other arithmetic  44.4 us (13%)
  matrix products  39.6 us (12%)
  starting transfers between devices  26.7 us (8%)
  between operations  14.9 us (4%)
    all_gather x1, waiting for transfers between devices, in_one_piece(): lax.all_gather(both, axis, axis=dim, tiled=True)  63.8 us
    all_to_all x1, waiting for transfers between devices, on_device(): lax.all_to_all(place_rows(stored_memories, row_slot, buffer_rows), 'req',...  46.6 us
    all_to_all x1, waiting for transfers between devices, side_by_side(): lax.all_to_all(both, axis, split_axis=split_dim, concat_axis=concat_dim,...  34.4 us
    dot_general x2, matrix products, advance(): jnp.einsum('nshi,nshj->nhij', carried, value_portion, precision=highest)  15 us
    all_to_all x1, starting transfers between devices, on_device(): lax.all_to_all(place_rows(previous_token_store, row_slot, buffer_rows), '...  13.4 us
    dot_general x3, matrix products, add_rows(): return jnp.dot(source, weight_piece, preferred_element_type=jnp.float32)  12.3 us
    convert_element_type x1, other arithmetic, mixed_input(): return (current + (previous - current) * blend_fractions[branch]).astype(...  11.7 us
    scatter x4, local copies, waits for them, and re-layouts, place_rows(): return blank.at[position].set(source)  9.1 us
  transfers between devices with their start and end apart: 5, of which 4 were waited for; matrix products, arithmetic and copies ran while one was open for 15% of the time, Pallas kernels for 0%

commit v1 on v0

v1 whole, which is shorter than its diff:
```python
import jax
import jax.numpy as jnp
from jax import lax
from jax.experimental import pallas as pl
from jax.experimental.pallas import tpu as pltpu
from jax.sharding import PartitionSpec as P

F32, BF16 = jnp.float32, jnp.bfloat16
HIGHEST = lax.Precision.HIGHEST
ROWS, LENGTH, WIDTH, TEAMS, TEAM_BREADTH = 32, 16, 256, 4, 64
TOKENS = ROWS * LENGTH
EPS = 0.00064


def mm(a, b):
    return lax.dot_general(a, b, (((1,), (0,)), ((), ())), preferred_element_type=F32)


def mm_nt(a, b):
    return lax.dot_general(a, b, (((1,), (1,)), ((), ())), preferred_element_type=F32)


def mm_tn(a, b, precision=None):
    return lax.dot_general(a, b, (((0,), (0,)), ((), ())), preferred_element_type=F32, precision=precision)


def take(ref, rows):
    return jnp.concatenate([ref[0, rows, :], ref[1, rows, :]], axis=1)


def put(ref, rows, value):
    ref[0, rows, :] = value[:, :128]
    ref[1, rows, :] = value[:, 128:]


def iota(shape, dim):
    return lax.broadcasted_iota(jnp.int32, shape, dim)


def recurrence_kernel(
    slot_ref, r_ref, k_ref, v_ref, low_ref, up_ref, base_ref, reward_ref, gain_ref, extent_ref, state_ref, token_ref,
    out_ref, state_out, shift_out,
    rp, kp, vf, dl, y, rin, kout, decay_all,
):
    a = iota((WIDTH, WIDTH), 0)
    target = (a & 1) * 128 + ((a >> 1) & 31) * 4 + (a >> 6)
    moved = iota((WIDTH, WIDTH), 1) == target
    perm = jnp.where(moved, 1.0, 0.0).astype(BF16)
    perm_f = jnp.where(moved, 1.0, 0.0)
    rp[...] = mm(r_ref[...], perm)
    kp[...] = mm(k_ref[...], perm)
    put(vf, slice(None), v_ref[...].astype(F32))
    row8 = iota((8, WIDTH), 0)
    both = jnp.where(row8 == 0, base_ref[...], jnp.where(row8 == 1, reward_ref[...], 0.0))
    both = lax.dot_general(both, perm_f, (((1,), (0,)), ((), ())), preferred_element_type=F32, precision=HIGHEST)
    base, reward = both[0:1], both[1:2]
    dl[...] = mm(low_ref[...], mm(up_ref[...], perm).astype(BF16)) + base
    out_ref[...] = jnp.zeros_like(out_ref)

    extent = jnp.broadcast_to(extent_ref[:, 0:1], (ROWS, WIDTH))
    last = jnp.zeros((ROWS, WIDTH), F32)
    for t in range(LENGTH):
        last = jnp.where(extent == t + 1, token_ref[t * ROWS : (t + 1) * ROWS].astype(F32), last)
    shift_out[...] = last.astype(BF16)

    lane = iota((1, WIDTH), 1)
    ri, ci = iota((128, 128), 0), iota((128, 128), 1)
    same = (ri & 7) == (ci & 7)
    rt, ct = ri >> 3, ci >> 3

    @pl.loop(0, ROWS // 8)
    def group(g):
        at = pl.multiple_of(g * 8, 8)

        def rows_of(ref):
            return [ref[pl.ds(pl.multiple_of(t * ROWS + at, 8), 8), :] for t in range(LENGTH)]

        ext = jnp.broadcast_to(extent_ref[pl.ds(at, 8), 0:1], (8, WIDTH))
        d = [jnp.where(ext > t, -jnp.exp(x), 0.0) for t, x in enumerate(rows_of(dl))]
        r = rows_of(rp)
        k = [jnp.where(ext > t, x, 0.0) for t, x in enumerate(rows_of(kp))]
        vals = [take(vf, pl.ds(pl.multiple_of(t * ROWS + at, 8), 8)) for t in range(LENGTH)]
        vals = jnp.concatenate(vals, axis=0).astype(BF16)
        totals, before, after = list(d), [None] * LENGTH, [None] * LENGTH

        def scaled(x, e):
            return x if e is None else x * jnp.exp(e)

        def stack(xs):
            return jnp.concatenate(xs, axis=0).astype(BF16)

        def scores(left, right, keep, so_far):
            right = stack(right)
            left = stack(left)
            res = []
            for h in range(TEAMS):
                s = mm_nt(jnp.where((lane & 3) == h, left, jnp.zeros((), BF16)), right)
                s = jnp.where(keep, s, 0.0)
                res.append(s if so_far is None else so_far[h] + s)
            return res

        total = scores([x * reward for x in r], k, same & (rt == ct), None)
        size = 1
        while size < LENGTH:
            late = [scaled(r[t], before[t]) if (t // size) & 1 else r[t] for t in range(LENGTH)]
            early = [k[t] if (t // size) & 1 else scaled(k[t], after[t]) for t in range(LENGTH)]
            sh = size.bit_length()
            keep = same & ((rt >> sh) == (ct >> sh)) & ((rt & size) != 0) & ((ct & size) == 0)
            total = scores(late, early, keep, total)
            for t in range(LENGTH):
                b = t // size
                if b & 1:
                    before[t] = totals[b - 1] if before[t] is None else before[t] + totals[b - 1]
                else:
                    after[t] = totals[b + 1] if after[t] is None else after[t] + totals[b + 1]
            totals = [totals[2 * b] + totals[2 * b + 1] for b in range(len(totals) // 2)]
            size *= 2
        mixed = None
        for h in range(TEAMS):
            part = mm(total[h].astype(BF16), jnp.where((lane >> 6) == h, vals, jnp.zeros((), BF16)))
            mixed = part if mixed is None else mixed + part
        for t in range(LENGTH):
            where = pl.ds(pl.multiple_of(t * ROWS + at, 8), 8)
            put(y, where, mixed[t * 8 : (t + 1) * 8])
            put(rin, where, scaled(r[t], before[t]))
            put(kout, where, scaled(k[t], after[t]))
        put(decay_all, pl.ds(at, 8), jnp.exp(totals[0]))

    lane128 = iota((LENGTH, 128), 1)
    low_half = lane128 < 64
    row_8, lane_8 = iota((8, 128), 0), iota((8, 128), 1)
    picks = jnp.where(((row_8 == 0) & (lane_8 < 64)) | ((row_8 == 1) & (lane_8 >= 64)), 1.0, 0.0)

    def spread(x):
        pieces = []
        for p in range(2):
            piece = x[p]
            for h in range(TEAMS):
                pieces.append(jnp.where((lane128 & 3) == h, piece, 0.0))
        return jnp.concatenate(pieces, axis=0).astype(BF16)

    def one_row(n, carry):
        where = pl.ds(n, LENGTH, stride=ROWS)
        state = state_ref[n]
        halves = []
        o = mm(spread([rin[p, where, :] for p in range(2)]), state)
        part = lambda p, h: o[(p * 4 + h) * 16 : (p * 4 + h + 1) * 16]
        for e in range(2):
            direct = jnp.where(low_half, part(0, 2 * e), part(1, 2 * e + 1))
            crossed = jnp.where(low_half, part(0, 2 * e + 1), part(1, 2 * e))
            halves.append(direct + pltpu.roll(crossed, 64, 1))
        for e in range(2):
            y[e, where, :] = y[e, where, :] + halves[e]
        keys = spread([kout[p, where, :] for p in range(2)])
        pieces = [None] * 8
        for e in range(2):
            v = vf[e, where, :]
            vr = pltpu.roll(v, 64, 1)
            pieces[2 * e] = jnp.where(low_half, v, 0.0)
            pieces[2 * e + 1] = jnp.where(low_half, vr, 0.0)
            pieces[4 + 2 * e] = jnp.where(low_half, 0.0, vr)
            pieces[4 + 2 * e + 1] = jnp.where(low_half, 0.0, v)
        update = mm_tn(keys, jnp.concatenate(pieces, axis=0).astype(BF16))
        e0, e1 = decay_all[0, pl.ds(n, 1), :], decay_all[1, pl.ds(n, 1), :]
        kept = mm_tn(jnp.where(row_8 == 0, e0, jnp.where(row_8 == 1, e1, 0.0)), picks, HIGHEST)
        state_out[n] = (kept * state.astype(F32) + update).astype(BF16)
        return carry

    lax.fori_loop(0, ROWS, one_row, 0, unroll=2)

    ones = jnp.where((iota((WIDTH, WIDTH), 0) >> 6) == (iota((WIDTH, WIDTH), 1) >> 6), 1.0 / TEAM_BREADTH, 0.0).astype(BF16)

    @pl.loop(0, 4)
    def norm(b):
        where = pl.ds(pl.multiple_of(b * 128, 128), 128)
        x = take(y, where)
        hi = x.astype(BF16)
        mean = mm(hi, ones) + mm((x - hi.astype(F32)).astype(BF16), ones)
        center = x - mean
        sq = center * center
        shi = sq.astype(BF16)
        var = mm(shi, ones) + mm((sq - shi.astype(F32)).astype(BF16), ones)
        normed = center * lax.rsqrt(var + EPS) * gain_ref[...]
        for j in range(4):
            alive = jnp.where(extent > b * 4 + j, normed[j * 32 : (j + 1) * 32], 0.0)
            put(y, pl.ds(pl.multiple_of(b * 128 + j * 32, 32), 32), alive)

    def place(n, carry):
        where = pl.ds(n, LENGTH, stride=ROWS)
        for e in range(2):
            out_ref[slot_ref[n], :, e * 128 : (e + 1) * 128] = y[e, where, :].astype(BF16)
        return carry

    lax.fori_loop(0, ROWS, place, 0, unroll=4)


def recurrence(slots, r, k, v, low, up, base, reward, gain, extents, state, tokens, interpret=False):
    vm = pl.BlockSpec(memory_space=pltpu.VMEM)
    big, split = pltpu.VMEM((TOKENS, WIDTH), F32), pltpu.VMEM((2, TOKENS, 128), F32)
    return pl.pallas_call(
        recurrence_kernel,
        out_shape=(
            jax.ShapeDtypeStruct((2 * ROWS, LENGTH, WIDTH), BF16),
            jax.ShapeDtypeStruct((ROWS, 128, 128), BF16),
            jax.ShapeDtypeStruct((ROWS, WIDTH), BF16),
        ),
        in_specs=[pl.BlockSpec(memory_space=pltpu.SMEM)] + [vm] * 11,
        out_specs=(vm, vm, vm),
        scratch_shapes=[big, big, split, big, split, split, split] + [pltpu.VMEM((2, ROWS, 128), F32)],
        name="recurrence",
        interpret=interpret,
    )(slots, r, k, v, low, up, base.reshape(1, WIDTH), reward.reshape(1, WIDTH), gain.reshape(1, WIDTH), extents, state, tokens)

MESH = pl.DeviceIdType.MESH
GROUPS, PARTS, XS, ZS, YS = 32, 16, 4, 8, 8
BLOCK = (LENGTH + 1) * ROWS
DEPTH = 128


def plan():
    copies = {}
    for d in (1, -1):
        for s in range(4):
            copies["kz", d, 0, s] = (("z", d), 128 if s < 3 else 64, [("kz", d, 0, s - 1)] if s else [])
        for q in range(-3, 5):
            need = [("kz", 1, 0, 3), ("kz", -1, 0, 3)] if q == 4 else [] if q == 0 else [("kz", -1 if q > 0 else 1, 0, abs(q) - 1)]
            copies["kx", d, q, 0] = (("x", d), 128, need)
            copies["kx", d, q, 1] = (("x", d), 64, [("kx", d, q, 0)])
        for s in range(2):
            copies["rx", d, 0, s] = (("x", d), 64 if s == 0 else 32, [("rx", d, 0, 0)] if s else [])
        for q in (0, -1, 1, 2):
            first = [("rx", 1, 0, 1), ("rx", -1, 0, 1)] if q == 2 else [] if q == 0 else [("rx", -q, 0, 0)]
            for s in range(4):
                copies["rz", d, q, s] = (("z", d), 64 if s < 3 else 32, [("rz", d, q, s - 1)] if s else first)
        for s in range(4):
            for half in range(2):
                if s == 3 and (half == 0) != (d == 1):
                    continue
                copies["ty", d, half, s] = (("y", d), 136, [("ty", d, half, s - 1)] if s else ["tokens"])
                copies["tc", d, half, s] = (("c", 0), 136, [("ty", d, half, s)])
    for half in range(2):
        copies["tc", 0, half, 0] = (("c", 0), 136, ["tokens"])
    return copies


def schedule(copies):
    rate = {"x": 46.0, "z": 46.0, "y": 46.0, "c": 200.0}
    free = {}
    for axis, busy in (("x", 7.0), ("z", 13.0), ("y", 0.0)):
        for d in (1, -1):
            free[axis, d] = busy
    free["c", 0] = 0.0
    lands, done, issued, steps = {"tokens": 16.0}, set(), set(), []

    def issue(now):
        for name, ((axis, d), size, need) in copies.items():
            if name not in issued and all(n in done for n in need):
                issued.add(name)
                start = max(now, free[axis, d])
                free[axis, d] = start + size * 1.024 / rate[axis]
                lands[name] = free[axis, d] + 1.5
                steps.append(("send", name))

    now = 1.0
    issue(now)
    while len(done) < len(copies) + 1:
        name = min((n for n in lands if n not in done), key=lambda n: lands[n])
        now = max(now, lands[name])
        done.add(name)
        steps.append(("arrive", name))
        issue(now)
    return steps


def gather_kernel(
    source_ref, row_ref, suffix_ref, shift_ref, wr_ref, wk_ref, wv_ref, blend_ref, down_ref,
    r_out, k_out, v_out, low_out, token_out,
    outbox, inbox, rows_f, tok, w, mixed, mixed_low, acc, low_acc,
    own_sem, swap_send, swap_recv, send_sem, recv_sem,
):
    me, part = lax.axis_index("req"), lax.axis_index("head")
    z, x = me // XS, me % XS
    yy, core = part // 2, part % 2

    def group_at(dz, dx):
        return ((z + dz + ZS) % ZS) * XS + (x + dx + XS) % XS

    def part_at(dy):
        return ((yy + dy + YS) % YS) * 2 + core

    partner = part + 1 - 2 * core

    own = []
    for q, ref in enumerate((wr_ref, wk_ref, wv_ref)):
        own.append(pltpu.make_async_copy(ref, w.at[q, pl.ds(pl.multiple_of(me * DEPTH, DEPTH), DEPTH)], own_sem.at[q]))
    for c in own:
        c.start()

    barrier = pltpu.get_barrier_semaphore()

    def greet(i, carry):
        pl.semaphore_signal(barrier, inc=1, device_id={"req": (me + i) % GROUPS}, device_id_type=MESH)
        return carry

    lax.fori_loop(1, GROUPS, greet, 0)
    for other in (part_at(1), part_at(-1), partner):
        pl.semaphore_signal(barrier, inc=1, device_id={"head": other}, device_id_type=MESH)

    def pack(i, carry):
        outbox[i] = suffix_ref[source_ref[i]]
        return carry

    lax.fori_loop(0, 2 * GROUPS, pack, 0, unroll=4)
    pl.semaphore_wait(barrier, GROUPS + 2)

    def swap(i):
        to = (me + i) % GROUPS
        return pltpu.make_async_remote_copy(
            src_ref=outbox.at[pl.ds(2 * to, 2)], dst_ref=inbox.at[pl.ds(2 * me, 2)],
            send_sem=swap_send.at[i], recv_sem=swap_recv.at[i], device_id={"req": to}, device_id_type=MESH,
        )

    def swap_in(i):
        source = inbox.at[pl.ds(2 * ((me - i + GROUPS) % GROUPS), 2)]
        return pltpu.make_async_remote_copy(
            src_ref=source, dst_ref=source, send_sem=swap_send.at[i], recv_sem=swap_recv.at[i],
            device_id={"req": (me + i) % GROUPS}, device_id_type=MESH,
        )

    def swap_start(i, carry):
        swap(i).start()
        return carry

    lax.fori_loop(1, GROUPS, swap_start, 0)
    for i in range(2):
        inbox[2 * me + i] = outbox[2 * me + i]
    for c in own:
        c.wait()

    def weight_rows(group, half):
        at = pl.multiple_of(group * DEPTH, DEPTH)
        if half is None:
            return pl.ds(at, DEPTH)
        return pl.ds(pl.multiple_of(at + half * 64, 64), 64)

    def place(name, arrival):
        kind, d, q, s = name
        back = d if arrival else 0
        half = 0 if d == 1 else 1
        if kind == "kz":
            return w.at[1:3, weight_rows(group_at(-d * s - back, 0), half if s == 3 else None)], {"req": group_at(d, 0)}
        if kind == "kx":
            return w.at[1:3, weight_rows(group_at(q, -d * s - back), half if s else None)], {"req": group_at(0, d)}
        if kind == "rx":
            return w.at[0, weight_rows(group_at(0, -d * s - back), half if s else None)], {"req": group_at(0, d)}
        if kind == "rz":
            return w.at[0, weight_rows(group_at(-d * s - back, q), half if s == 3 else None)], {"req": group_at(d, 0)}
        piece = pl.ds(q * (BLOCK // 2), BLOCK // 2)
        if kind == "ty":
            return tok.at[part_at(-d * s - back), piece], {"head": part_at(d)}
        source = part_at(-d * (s + 1)) if d else part
        if arrival:
            source = source + 1 - 2 * core
        return tok.at[source, piece], {"head": partner}

    copies = plan()
    number = {name: i for i, name in enumerate(copies)}

    def copy(name, arrival):
        ref, device = place(name, arrival)
        i = number[name]
        return pltpu.make_async_remote_copy(
            src_ref=ref, dst_ref=ref, send_sem=send_sem.at[i], recv_sem=recv_sem.at[i], device_id=device, device_id_type=MESH
        )

    def unpack():
        def wait(i, carry):
            swap_in(i).wait_recv()
            return carry

        lax.fori_loop(1, GROUPS, wait, 0)

        def row(n, carry):
            value = inbox[row_ref[n]].astype(F32)
            for e in range(2):
                rows_f[e, pl.ds(n, LENGTH, stride=ROWS), :] = value[:, e * 128 : (e + 1) * 128]
            return carry

        lax.fori_loop(0, ROWS, row, 0, unroll=4)
        tok[part, 0:ROWS] = shift_ref[...]
        tok[part, ROWS:BLOCK] = take(rows_f, slice(None)).astype(BF16)

    low_acc[...] = jnp.zeros_like(low_acc)

    def mix(source):
        columns = pl.ds(pl.multiple_of(source * WIDTH, WIDTH), WIDTH)
        blends = [blend_ref[q : q + 1, columns] for q in range(4)]

        def rows(i, carry):
            at = pl.ds(pl.multiple_of(i * 64, 64), 64)
            before = tok[source, at].astype(F32)
            now = tok[source, pl.ds(pl.multiple_of(i * 64 + ROWS, 32), 64)].astype(F32)
            change = before - now
            for q in range(3):
                mixed[q, at, columns] = (now + change * blends[q]).astype(BF16)
            mixed_low[at] = (now + change * blends[3]).astype(BF16)
            return carry

        lax.fori_loop(0, TOKENS // 64, rows, 0)
        low_acc[...] += mm(mixed_low[...], down_ref[columns])

    def project(q, out):
        acc[...] = jnp.zeros_like(acc)

        def rows(i, carry):
            at = pl.ds(pl.multiple_of(i * 512, 512), 512)
            acc[...] += mm(mixed[q, :, at], w[q, at])
            return carry

        lax.fori_loop(0, PARTS // 2, rows, 0)
        out[...] = acc[...].astype(BF16)

    arrived, pending = set(), []
    for verb, name in schedule(copies):
        if verb == "send":
            copy(name, False).start()
            continue
        if pending:
            mix(pending.pop(0))
        if name == "tokens":
            unpack()
            pending.append(part)
        else:
            copy(name, True).wait_recv()
        arrived.add(name)
        if name != "tokens" and name[0] in ("ty", "tc"):
            kind, d, half, s = name
            if kind == "tc" and d == 0:
                ready = {("tc", 0, 0, 0), ("tc", 0, 1, 0)} <= arrived
            elif s == 3:
                ready = {(kind, 1, 0, 3), (kind, -1, 1, 3)} <= arrived
            else:
                ready = {(kind, d, 0, s), (kind, d, 1, s)} <= arrived
            if ready:
                source = part if d == 0 else part_at(-d * (s + 1))
                pending.append(source if kind == "ty" else source + 1 - 2 * core)
    for source in pending:
        mix(source)
    low_out[...] = jnp.tanh(low_acc[...]).astype(BF16)
    token_out[...] = tok[part, ROWS:BLOCK]
    project(0, r_out)
    project(1, k_out)
    project(2, v_out)

    def drain(i, carry):
        swap(i).wait_send()
        return carry

    lax.fori_loop(1, GROUPS, drain, 0)
    for name in copies:
        copy(name, False).wait_send()


def gather(source, row, suffix, shift, wr, wk, wv, blend, down):
    vm, sm, hbm = (pl.BlockSpec(memory_space=s) for s in (pltpu.VMEM, pltpu.SMEM, pl.ANY))
    tokens = jax.ShapeDtypeStruct((TOKENS, WIDTH), BF16)
    count = len(plan())
    return pl.pallas_call(
        gather_kernel,
        out_shape=(tokens, tokens, tokens, jax.ShapeDtypeStruct((TOKENS, DEPTH), BF16), tokens),
        in_specs=[sm, sm, vm, vm, hbm, hbm, hbm, vm, vm],
        out_specs=(vm,) * 5,
        scratch_shapes=[
            pltpu.VMEM((2 * GROUPS, LENGTH, WIDTH), BF16),
            pltpu.VMEM((2 * GROUPS, LENGTH, WIDTH), BF16),
            pltpu.VMEM((2, TOKENS, 128), F32),
            pltpu.VMEM((PARTS, BLOCK, WIDTH), BF16),
            pltpu.VMEM((3, GROUPS * DEPTH, WIDTH), BF16),
            pltpu.VMEM((3, TOKENS, PARTS * WIDTH), BF16),
            pltpu.VMEM((TOKENS, WIDTH), BF16),
            pltpu.VMEM((TOKENS, WIDTH), F32),
            pltpu.VMEM((TOKENS, DEPTH), F32),
            pltpu.SemaphoreType.DMA((3,)),
            pltpu.SemaphoreType.DMA((GROUPS,)),
            pltpu.SemaphoreType.DMA((GROUPS,)),
            pltpu.SemaphoreType.DMA((count,)),
            pltpu.SemaphoreType.DMA((count,)),
        ],
        compiler_params=pltpu.CompilerParams(collective_id=0, has_side_effects=True, vmem_limit_bytes=60000 * 1024),
        name="gather",
    )(source, row, suffix, shift, wr, wk, wv, blend, down)

def on_device(
    suffix_embeddings,
    suffix_extents,
    memory_line_pointer,
    previous_token_store,
    stored_memories,
    blend_fractions,
    acceptor_linear,
    address_linear,
    payload_linear,
    fading_baseline,
    fading_bottleneck_down,
    fading_bottleneck_up,
    self_reward,
    team_normalizer_gain,
):
    group = lax.axis_index("req")
    owners = (memory_line_pointer // ROWS).reshape(GROUPS, ROWS)
    earlier = jnp.arange(ROWS)[:, None] > jnp.arange(ROWS)[None, :]
    rank = jnp.sum(((owners[:, :, None] == owners[:, None, :]) & earlier[None]).astype(jnp.int32), axis=2)
    inbox_slot = (jnp.arange(GROUPS, dtype=jnp.int32)[:, None] * 2 + rank).reshape(-1)
    outbox_slot = lax.dynamic_index_in_dim(owners * 2 + rank, group, 0, keepdims=False)
    here = memory_line_pointer[None, :] == (group * ROWS + jnp.arange(ROWS, dtype=jnp.int32))[:, None]
    row_slot = jnp.sum(jnp.where(here, inbox_slot[None, :], 0), axis=1)
    row_extent = jnp.sum(jnp.where(here, suffix_extents[None, :], 0), axis=1)
    wanted = outbox_slot[None, :] == jnp.arange(2 * GROUPS, dtype=jnp.int32)[:, None]
    source = jnp.sum(jnp.where(wanted, jnp.arange(ROWS, dtype=jnp.int32)[None, :], 0), axis=1)
    r, k, v, low, tokens = gather(
        source, row_slot, suffix_embeddings, previous_token_store,
        acceptor_linear, address_linear, payload_linear, blend_fractions, fading_bottleneck_down,
    )
    state = stored_memories.reshape(ROWS, TEAMS, 32, 128).transpose(0, 2, 1, 3).reshape(ROWS, 128, 128)
    extents = jnp.broadcast_to(row_extent[:, None], (ROWS, 128))
    outbox, new_state, new_shift = recurrence(
        row_slot, r, k, v, low, fading_bottleneck_up, fading_baseline, self_reward, team_normalizer_gain, extents, state, tokens
    )
    inbox = lax.all_to_all(outbox, "req", split_axis=0, concat_axis=0, tiled=True)
    mixed_out = inbox[outbox_slot]
    new_state = new_state.reshape(ROWS, 32, TEAMS, 128).transpose(0, 2, 1, 3).reshape(ROWS, TEAMS, 4096)
    return (mixed_out, new_state, new_shift)


def solution(mesh):
    placed = (
        P("req", None, "head"),
        P(),
        P(),
        P("req", "head"),
        P("req", "head", None),
        P(),
        P("req", "head"),
        P("req", "head"),
        P("req", "head"),
        P("head"),
        P(),
        P(None, "head"),
        P("head"),
        P("head"),
    )
    return jax.shard_map(
        on_device,
        mesh=mesh,
        in_specs=placed,
        out_specs=(P("req", None, "head"), P("req", "head", None), P("req", "head")),
        check_vma=False,
    )
```

time: 338 us -> 122 us (0.36)
  the two profiles are of different devices: /device:TPU:4 before, /device:TPU:2 now
where the time goes in v1:
time: 122 us
  Pallas kernels  93.5 us (77%)
  waiting for transfers between devices  13.9 us (11%)
  starting transfers between devices  8.42 us (7%)
  local copies, waits for them, and re-layouts  3.38 us (3%)
  other arithmetic  2.23 us (2%)
    pallas_call x1, Pallas kernels, gather(): pl.pallas_call(gather_kernel, out_shape=(tokens, tokens, tokens, jax.Shap...  77.9 us
    pallas_call x1, Pallas kernels, recurrence(): pl.pallas_call(recurrence_kernel, out_shape=(jax.ShapeDtypeStruct((2 * RO...  15.6 us
    all_to_all x1, waiting for transfers between devices, on_device(): lax.all_to_all(outbox, 'req', split_axis=0, concat_axis=0, tiled=True)  13.9 us
    all_to_all x1, starting transfers between devices, on_device(): lax.all_to_all(outbox, 'req', split_axis=0, concat_axis=0, tiled=True)  8.42 us
  transfers between devices with their start and end apart: 1, of which 1 were waited for; matrix products, arithmetic and copies ran while one was open for 0% of the time, Pallas kernels for 0%

profile of v1, /device:TPU:2, one launch (start us, length us, event | category | flops | bytes accessed | tf_op | source)
XLA Modules:
  0.0 122.1 jit_solution(5024177677603860558)
XLA Ops:
  0.7 0.0 copy-start
  0.7 0.7 copy-done
  1.4 0.1 eq.46
  1.4 0.8 convert_reduce_fusion
  2.2 0.6 select_reduce_fusion.source_ref
  2.8 0.1 broadcast_add_fusion
  2.9 0.0 copy-start.1
  2.9 0.1 add.50
  3.0 0.6 copy-done.1
  3.6 0.7 fusion.1
  4.3 77.9 %gather.7 = (bf16[512,256]{1,0:T(8,128)(2,1)}, bf16[512,256]{1,0:T(8,128)(2,1)}, bf16[512,256]{1,0:T(8,128)(2,1)}, bf16[512,128]{1,0:T(8,128)(2,1)}, bf16[512,256]{1,0:T(8,128)(2,1)}) custom-call(s32[64]{0:T(128)} %select_reduce_fusion.source_ref, s32[32]{0:T(128)} %get-tuple-element.20.row_ref.slot_ref, bf16[32,16,256]{2,1,0:T(8,128)(2,1)} %suffix_ref.1, ...), custom_call_target="tpu_custom_call" | custom-call | tf_op jit(solution)/shard_map/gather/pallas_call | solution.py:468
  82.3 0.7 broadcast_in_dim.52.extent_ref
  83.0 15.6 %recurrence.1 = (bf16[64,16,256]{2,1,0:T(8,128)(2,1)}, bf16[32,128,128]{2,1,0:T(8,128)(2,1)}, bf16[32,256]{1,0:T(8,128)(2,1)}) custom-call(s32[32]{0:T(128)} %get-tuple-element.20.row_ref.slot_ref, bf16[512,256]{1,0:T(8,128)(2,1)} %get-tuple-element.11.r_ref, bf16[512,256]{1,0:T(8,128)(2,1)} %get-tuple-element.12.k_ref, ...), custom_call_target="tpu_custom_call" | custom-call | tf_op jit(solution)/shard_map/recurrence/pallas_call | solution.py:200
  98.5 8.4 %all-to-all-start = ((bf16[64,16,256]{2,1,0:T(8,128)(2,1)}), bf16[64,16,256]{2,1,0:T(8,128)(2,1)S(1)}, u32[]{:S(2)}, u32[]{:S(2)}) async-start(bf16[64,16,256]{2,1,0:T(8,128)(2,1)} %get-tuple-element.16), calls=%async_computation | async-start | bytes 1048576 | tf_op jit(solution)/shard_map/all_to_all | solution.py:529
  107.0 13.9 %all-to-all-done = bf16[64,16,256]{2,1,0:T(8,128)(2,1)S(1)} async-done(((bf16[64,16,256]{2,1,0:T(8,128)(2,1)}), bf16[64,16,256]{2,1,0:T(8,128)(2,1)S(1)}, u32[]{:S(2)}, u32[]{:S(2)}) %all-to-all-start) | async-done | bytes 524320 | tf_op jit(solution)/shard_map/all_to_all | solution.py:529
  120.8 1.3 %gather_fusion = bf16[32,16,256]{2,1,0:T(8,128)(2,1)} fusion(bf16[64,16,256]{2,1,0:T(8,128)(2,1)S(1)} %all-to-all-done, s32[1024]{0:T(1024)S(1)} %pad_clamp_fusion), kind=kCustom, calls=%fused_computation | custom fusion | bytes 524416 | tf_op jit(solution)/shard_map/gather | solution.py:530
  (6 shorter events, 0.0 us)
Async XLA Ops:
  0.7 0.7 copy-start
  2.9 0.7 copy-start.1
  98.5 22.3 %all-to-all-start = ((bf16[64,16,256]{2,1,0:T(8,128)(2,1)}), bf16[64,16,256]{2,1,0:T(8,128)(2,1)S(1)}, u32[]{:S(2)}, u32[]{:S(2)}) async-start(bf16[64,16,256]{2,1,0:T(8,128)(2,1)} %get-tuple-element.16), calls=%async_computation | async-start | bytes 1048576 | tf_op jit(solution)/shard_map/all_to_all | solution.py:529
